TPU v7x, 32 devices: a whole 2x2x4 slice. The times are simulated.
32 devices in a mesh: gx: 4 (over y, x), gy: 4 (over z), gz: 2 (over core).
Axes of the slice: x: 2, y: 2, z: 4, core: 2. Of those that a mesh axis runs over, the one named last changes fastest.
Arguments:
- positions: float32 [2048, 3, 128], P(('gx', 'gy', 'gz')), may hold values from 0 to 1
- charges: float32 [2048, 128], P(('gx', 'gy', 'gz')), may hold values from -0.18 to 0.18
- counts: int32 [2048], P(('gx', 'gy', 'gz')), may hold values from 1 to 128
- up_inverse: float32 [64, 64], replicated, may hold values from -0.09375 to 0.09375
- down_inverse: float32 [64, 64], replicated, may hold values from -0.09375 to 0.09375
- inner_surface: float32 [3, 64], replicated, may hold values from 0.15 to 0.85
- outer_surface: float32 [3, 64], replicated, may hold values from -1 to 2, as said below
Outputs:
- potential: float32 [2048, 128], P(('gx', 'gy', 'gz'))
Inputs may be any that keep to these rules, and one draw needn't show every extreme that they name: `outer_surface`: each point lies on the boundary of the cube [-1, 2]^3.
All inputs are finite; a program needn't handle non-finite values.
Results may differ from a plain program's by a relative error of at most 0.0003.
Values sent between devices are 32-bit elements; how exact they have to be, the bound alone decides.
A program may use at most 64 MiB of HBM per device.

v0:
```python
from functools import partial

import jax
import jax.numpy as jnp
from jax import lax
from jax.experimental import pallas as pl
from jax.experimental.pallas import tpu as pltpu
from jax.sharding import PartitionSpec as P

CX = 4
CY = 4
CZ = 4
PTS = 128
TERMS = 64
LEAF = CX * CY * CZ
EXT = (CX + 2) * (CY + 2) * (CZ + 2)
FEATS = 32
LINE = 8
PAIRS = 4
STEP = 16


SOFTEN = 0.0025
EXACT_DOTS = lax.Precision.HIGHEST


def iota(shape, dimension):
    return lax.broadcasted_iota(jnp.int32, shape, dimension)


def column(row):
    size = row.shape[1]
    eye = iota((size, size), 0) == iota((size, size), 1)
    return jnp.sum(jnp.where(eye, row, 0.0), axis=1, keepdims=True)


def over_plane(size_x, size_y, body, start, unroll=1):
    def line(x, carry):
        return lax.fori_loop(0, size_y, lambda y, held: body(x, y, held), carry, unroll=unroll)

    return lax.fori_loop(0, size_x, line, start)


def rounded(value):
    return value.astype(jnp.bfloat16).astype(jnp.float32)


def three_parts(value):
    high = rounded(value)
    middle = rounded(value - high)
    low = rounded(value - high - middle)
    return high, middle, low


def squares_of(points, shift_x, shift_y, shift_z, extra):
    row = iota((8, PTS), 0) % 4
    twice = jnp.concatenate([points, points], axis=0)
    place = twice + jnp.where(row == 0, shift_x, jnp.where(row == 1, shift_y, shift_z))
    square = place * place
    norm = square[0:1] + square[1:2] + square[2:3] + extra
    return jnp.where(row == 3, norm, place), row == 3, iota((8, PTS), 0) < 4


def source_features(points, spots):
    row = iota((8, PTS), 0)
    last, first = row % 4 == 3, row < 4
    both = jnp.concatenate(points, axis=0)
    shift = jnp.where(first, spots[0][2], spots[1][2])
    shift = jnp.where(row % 4 == 0, jnp.where(first, spots[0][0], spots[1][0]), shift)
    shift = jnp.where(row % 4 == 1, jnp.where(first, spots[0][1], spots[1][1]), shift)
    place = both + shift
    square = place * place
    norm = pltpu.roll(square, 1, 0) + pltpu.roll(square, 2, 0) + pltpu.roll(square, 3, 0)
    high, middle, low = three_parts(jnp.where(last, norm, -2.0 * place))
    high_one = jnp.where(last, 1.0, high)
    middle_one = jnp.where(last, 1.0, middle)
    pairs = ((high, middle), (low, high_one), (high_one, middle_one))
    blank = jnp.zeros((8, PTS), jnp.float32)
    lower = [jnp.where(first, one, pltpu.roll(two, 4, 0)) for one, two in pairs]
    upper = [jnp.where(first, pltpu.roll(one, 4, 0), two) for one, two in pairs]
    return [
        jnp.concatenate(rows + [blank], axis=0).astype(jnp.bfloat16) for rows in (lower, upper)
    ]


def target_features(points, shift_x, shift_y, shift_z):
    value, last, first = squares_of(points, shift_x, shift_y, shift_z, SOFTEN)
    high, middle, low = three_parts(value)
    high_one = jnp.where(last, 1.0, high)
    rows = [
        high_one,
        jnp.where(first, high_one, jnp.where(last, high, middle)),
        jnp.where(first, jnp.where(last, middle, low), jnp.where(last, low, middle)),
        jnp.zeros((8, PTS), jnp.float32),
    ]
    return jnp.transpose(jnp.concatenate(rows, axis=0)).astype(jnp.bfloat16)


def whole():
    return pl.BlockSpec(memory_space=pltpu.VMEM)


def scalars():
    return pl.BlockSpec(memory_space=pltpu.SMEM)


def anywhere():
    return pl.BlockSpec(memory_space=pl.ANY)


def axis_bits():
    low_bits = lax.axis_size("gz").bit_length() - 1
    mid_bits = lax.axis_size("gy").bit_length() - 1
    high_bits = lax.axis_size("gx").bit_length() - 1
    return (low_bits, mid_bits, high_bits)


SIDES = [
    (x, y, z)
    for x in (-1, 0, 1)
    for y in (-1, 0, 1)
    for z in (-1, 0, 1)
    if (x, y, z) != (0, 0, 0)
]


def rim(side, size, layers):
    if side > 0:
        return pl.ds(size, layers), pl.ds(0, layers)
    if side < 0:
        return pl.ds(layers, layers), pl.ds(size + layers, layers)
    return pl.ds(layers, size), pl.ds(layers, size)


def middle(cell):
    if isinstance(cell, int):
        return jnp.float32(cell) - (CX // 2 + 1)
    return cell.astype(jnp.float32) - (CX // 2 + 1)


def ext_index(x, y, z):
    return ((x + 1) * (CY + 2) + y + 1) * (CZ + 2) + z + 1


def clear_part(grouped, surface):
    def one(n, carry):
        grouped[n] = jnp.zeros((8, 16, 2 * TERMS), jnp.bfloat16)
        return carry

    lax.fori_loop(0, 64, one, 0)
    surface[...] = jnp.zeros((4, PTS), jnp.float32)


def upward_part(pos, charge, count, up, outer, masked, turned, wide_points, wide_dens, order_ref):
    row = count[...].astype(jnp.float32)
    counted = column(row)
    masked[...] = jnp.where(
        iota((LEAF, PTS), 1).astype(jnp.float32) < counted, charge[...], 0.0
    )
    spots = [jnp.broadcast_to(column(outer[c : c + 1, :]), (TERMS, PTS)) for c in range(3)]
    lanes = iota((TERMS, PTS), 1)

    def leaf(n, check):
        source = masked[pl.ds(n, 1), :]
        square = jnp.full((TERMS, PTS), SOFTEN, jnp.float32)
        for c in range(3):
            spread = spots[c] - pos[c, pl.ds(n, 1), :]
            square = square + spread * spread
        total = jnp.sum(lax.rsqrt(square) * source, axis=1, keepdims=True)
        return jnp.where(lanes == n, total, check)

    check = lax.fori_loop(0, LEAF, leaf, jnp.zeros((TERMS, PTS), jnp.float32), unroll=16)
    dens = jnp.dot(up[...], check, preferred_element_type=jnp.float32, precision=EXACT_DOTS)
    turned[...] = jnp.transpose(jnp.concatenate([dens, dens], axis=0))
    even = turned[pl.ds(0, LEAF // 2, stride=2), :]
    odd = turned[pl.ds(1, LEAF // 2, stride=2), :]
    both = jnp.where(iota((LEAF // 2, PTS), 1) < TERMS, even, odd)
    for m in range(LEAF // 2):
        x, y, z = m // (CY * CZ // 2), m // (CZ // 2) % CY, m % (CZ // 2)
        wide_dens[x + 2, y + 2, z + 1] = both[m : m + 1]
    return row, counted


def points_part(pos, masked, wide_points):
    def line(x, y, carry):
        for z in range(CZ):
            n = (x * CY + y) * CZ + z
            rows = [pos[c, pl.ds(n, 1), :] for c in range(3)] + [masked[pl.ds(n, 1), :]]
            wide_points[x + 1, y + 1, z + 1] = jnp.concatenate(rows, axis=0)
        return carry

    over_plane(CX, CY, line, 0, CY)


def order_part(row, counted, order_ref):
    leaf = iota((LEAF, LEAF), 0).astype(jnp.float32)
    other = iota((LEAF, LEAF), 1).astype(jnp.float32)
    mine = counted * LEAF + leaf
    theirs = row * LEAF + other
    rank = jnp.sum(jnp.where(theirs < mine, 1.0, 0.0), axis=1, keepdims=True)
    order = jnp.sum(jnp.where(rank == other, leaf, 0.0), axis=0, keepdims=True)
    order_ref[...] = jnp.concatenate([order, row], axis=1).astype(jnp.int32)


def weights_part(inner, weights):
    upper_lanes = iota((TERMS, 2 * TERMS), 1) >= TERMS
    spread = []
    for c in range(3):
        row = inner[c : c + 1, :]
        spread.append(jnp.concatenate([row, row], axis=1) - column(row))
    squares_z = []
    for pair in range(PAIRS):
        shift = jnp.where(upper_lanes, float(pair + 1), float(pair - 3))
        squares_z.append((spread[2] - shift) * (spread[2] - shift))

    def line(n_x, n_y, carry):
        shift_x = n_x - 3
        shift_y = n_y - 3
        d_x = spread[0] - shift_x.astype(jnp.float32)
        d_y = spread[1] - shift_y.astype(jnp.float32)
        plane = d_x * d_x + d_y * d_y + SOFTEN
        close = jnp.maximum(jnp.abs(shift_x), jnp.abs(shift_y)) < 2
        for pair in range(PAIRS):
            weight = lax.rsqrt(plane + squares_z[pair])
            if pair == 0:
                weight = jnp.where(close & upper_lanes, 0.0, weight)
            if pair >= 2:
                weight = jnp.where(close & ~upper_lanes, 0.0, weight)
            high = weight.astype(jnp.bfloat16)
            low = (weight - high.astype(jnp.float32)).astype(jnp.bfloat16)
            at = (n_x * 7 + n_y) * 2
            weights[at, pair * TERMS : (pair + 1) * TERMS] = high
            weights[at + 1, pair * TERMS : (pair + 1) * TERMS] = low
        return carry

    over_plane(7, 7, line, 0, 7)


def gather_part(wide_dens, raw, grouped):
    half = iota((8, 2 * TERMS), 1) < TERMS
    blank = jnp.zeros((8, 2 * TERMS), jnp.float32)

    def line(a_x, a_y, carry):
        whole_rows = []
        for b in range(3):
            at = a_x * 18 + a_y * 3 + b
            for parent in range(8):
                cell_x = 2 * (parent // 4) + a_x
                cell_y = 2 * (parent // 2 % 2) + a_y
                raw[at, parent : parent + 1, :] = wide_dens[cell_x, cell_y, parent % 2 + b]
        for b in range(3):
            value = raw[a_x * 18 + a_y * 3 + b]
            high = rounded(value)
            whole_rows.append((high, value - high))
        for part in range(2):
            first, second, third = (member[part] for member in whole_rows)
            one, two, three = (pltpu.roll(member, TERMS, 1) for member in (first, second, third))
            tiles = [
                (jnp.where(half, 0.0, one), first),
                (jnp.where(half, one, two), second),
                (jnp.where(half, two, three), third),
                (jnp.where(half, three, 0.0), blank),
            ]
            for at, rows in enumerate(tiles):
                grouped[(a_x + 1) * 8 + a_y + 1, 4 * part + at] = jnp.concatenate(
                    rows, axis=0
                ).astype(jnp.bfloat16)
        return carry

    lax.fori_loop(
        0, 6, lambda x, held: lax.fori_loop(0, 6, lambda y, kept: line(x, y, kept), held, unroll=6), 0, unroll=6
    )


def translate_part(weights, grouped, down_ref, local):
    def product(places, parities):
        lefts = []
        rights = []
        for n_x, n_y in places:
            for lanes in range(2):
                pieces = []
                for kind in (0, 4, 2, 6):
                    for parity in parities:
                        at = (n_x + parity // 2) * 8 + n_y + parity % 2
                        pieces.append(grouped[at, kind + lanes])
                lefts.append(jnp.concatenate(pieces, axis=0))
            at = (n_x * 7 + n_y) * 2
            rights.append(jnp.concatenate([weights[at], weights[at + 1]], axis=1))
        result = jnp.dot(
            jnp.concatenate(lefts, axis=1),
            jnp.concatenate(rights, axis=0),
            preferred_element_type=jnp.float32,
        )
        for kind in range(4):
            for k, parity in enumerate(parities):
                at = (kind * len(parities) + k) * 16
                sums[kind * 4 + parity].append(result[at : at + 16])

    sums = [[] for _ in range(16)]
    inner_shifts = range(1, 6)
    product([(n_x, n_y) for n_x in inner_shifts for n_y in inner_shifts], (0, 1, 2, 3))
    product([(0, n_y) for n_y in range(7)], (2, 3))
    product([(6, n_y) for n_y in range(7)], (0, 1))
    product([(n_x, 0) for n_x in inner_shifts], (1, 3))
    product([(n_x, 6) for n_x in inner_shifts], (0, 2))
    total = jnp.concatenate([sum(rows[1:], rows[0]) for rows in sums], axis=0)
    total = total[:, : 2 * TERMS] + total[:, 2 * TERMS :]
    lower = total[:LEAF] + total[LEAF : 2 * LEAF]
    upper = total[2 * LEAF : 3 * LEAF] + total[3 * LEAF :]
    total = jnp.where(iota((LEAF, 2 * TERMS), 1) < TERMS, lower, upper)
    down = down_ref[...]
    down = jnp.concatenate([down, down], axis=1)
    down = jnp.concatenate([down, jnp.zeros_like(down)], axis=0)
    local[...] = lax.dot_general(
        total,
        down,
        (((1,), (1,)), ((), ())),
        preferred_element_type=jnp.float32,
        precision=EXACT_DOTS,
    )


def gather_body(
    pos_hbm,
    charge_hbm,
    count_hbm,
    up_hbm,
    down_hbm,
    inner_hbm,
    outer_hbm,
    wide_points,
    sources,
    targets,
    local,
    order_ref,
    wide_dens,
    pos,
    charge,
    count,
    up,
    down,
    inner,
    outer,
    masked,
    turned,
    weights,
    raw,
    grouped,
    surface,
    order_rows,
    load_sem,
    send_sem,
    recv_sem,
):
    low_bits, mid_bits, high_bits = axis_bits()
    total_bits = low_bits + mid_bits + high_bits
    device = (
        lax.axis_index("gx") * 2**mid_bits + lax.axis_index("gy")
    ) * 2**low_bits + lax.axis_index("gz")
    place = []
    extent = []
    for c in range(3):
        bits = list(range(c, total_bits, 3))
        place.append(sum(((device >> bit) & 1) * 2**rank for rank, bit in enumerate(bits)))
        extent.append(2 ** len(bits))

    steps = []
    for c in range(3):
        moves = {}
        for move in (-1, 0, 1):
            moved = place[c] + move
            spot = [0, 0, 0]
            for rank, bit in enumerate(range(c, total_bits, 3)):
                digit = (moved >> rank) & 1
                if bit < low_bits:
                    spot[2] = spot[2] + digit * 2**bit
                elif bit < low_bits + mid_bits:
                    spot[1] = spot[1] + digit * 2 ** (bit - low_bits)
                else:
                    spot[0] = spot[0] + digit * 2 ** (bit - low_bits - mid_bits)
            moves[move] = spot
        steps.append(moves)
    room = [{1: place[c] < extent[c] - 1, -1: place[c] > 0} for c in range(3)]
    inside = {}
    for side in SIDES:
        held = None
        for c in range(3):
            if side[c] != 0:
                held = room[c][side[c]] if held is None else held & room[c][side[c]]
        inside[side] = held

    def there(side):
        return inside[side]

    def coordinates(side):
        return tuple(
            sum(steps[c][side[c]][axis] for c in range(3)) + jnp.int32(0) for axis in range(3)
        )

    kinds = (
        (wide_dens, (CX, CY, CZ // 2), (2, 2, 1)),
        (wide_points, (CX, CY, CZ), (1, 1, 1)),
    )

    def regions(kind, at):
        wide, sizes, layers = kinds[kind]
        return zip(*(rim(SIDES[at][c], sizes[c], layers[c]) for c in range(3)))

    def remote(kind, at):
        wide = kinds[kind][0]
        source, target = regions(kind, at)
        return pltpu.make_async_remote_copy(
            src_ref=wide.at[source],
            dst_ref=wide.at[target],
            send_sem=send_sem.at[kind, at],
            recv_sem=recv_sem.at[kind, at],
            device_id=coordinates(SIDES[at]),
            device_id_type=pl.DeviceIdType.MESH,
        )

    loads = [
        pltpu.make_async_copy(source, target, load_sem.at[at])
        for at, (source, target) in enumerate(
            (
                (pos_hbm, pos),
                (charge_hbm, charge),
                (count_hbm, count),
                (outer_hbm, outer),
                (up_hbm, up),
                (inner_hbm, inner),
                (down_hbm, down),
            )
        )
    ]
    for load in loads:
        load.start()
    barrier = pltpu.get_barrier_semaphore()
    met = jnp.int32(0)
    order = sorted(range(len(SIDES)), key=lambda at: -sum(map(abs, SIDES[at])))
    for at in order:
        met = met + jnp.where(there(SIDES[at]), 1, 0)

        @pl.when(there(SIDES[at]))
        def _(at=at):
            pl.semaphore_signal(
                barrier,
                inc=1,
                device_id=coordinates(SIDES[at]),
                device_id_type=pl.DeviceIdType.MESH,
            )

    clear_part(grouped, surface)
    for load in loads:
        load.wait()
    surface[0:3, 0:TERMS] = outer[...]
    row, counted = upward_part(
        pos, charge, count, up, outer, masked, turned, wide_points, wide_dens, order_ref
    )
    pl.semaphore_wait(barrier, met)

    def send(kind):
        for at in order:

            @pl.when(there(SIDES[at]))
            def _(at=at):
                remote(kind, at).start()

    def sent(kind):
        for at in order:

            @pl.when(there(SIDES[at]))
            def _(at=at):
                remote(kind, at).wait_send()

    def finish(kind):
        for at in order:

            @pl.when(there(tuple(-c for c in SIDES[at])))
            def _(at=at):
                remote(kind, at).wait_recv()

    def blank(kind):
        for at in order:

            @pl.when(~there(tuple(-c for c in SIDES[at])))
            def _(at=at):
                wide = kinds[kind][0]
                _, target = regions(kind, at)
                shape = tuple(piece.size for piece in target) + wide.shape[3:]
                wide[target] = jnp.zeros(shape, jnp.float32)

    send(0)
    points_part(pos, masked, wide_points)
    send(1)
    order_part(row, counted, order_rows)
    ordering = pltpu.make_async_copy(order_rows, order_ref, load_sem.at[7])
    ordering.start()
    blank(0)
    blank(1)
    weights_part(inner, weights)

    def source(e_x, e_y, e_z, other):
        base = (e_x * (CY + 2) + e_y) * (CZ + 2)
        made = source_features(
            [wide_points[e_x, e_y, at] for at in (e_z, other)],
            [(middle(e_x), middle(e_y), middle(at)) for at in (e_z, other)],
        )
        for at, features in zip((e_z, other), made):
            sources[base + at] = features

    def prepare_own(x, y, carry):
        for z in range(0, CZ, 2):
            source(x + 1, y + 1, z + 1, z + 2)
            n = (x * CY + y) * CZ + z
            spots = [(middle(x + 1), middle(y + 1), middle(z + k + 1)) for k in range(2)]
            for k, features in enumerate(source_features([surface[...]] * 2, spots)):
                sources[EXT + n + k] = features
            for k in range(2):
                points = wide_points[x + 1, y + 1, z + k + 1]
                targets[n + k] = target_features(points, *spots[k])
        return carry

    over_plane(CX, CY, prepare_own, 0, CY)
    ordering.wait()
    sent(0)
    finish(0)
    gather_part(wide_dens, raw, grouped)
    translate_part(weights, grouped, down, local)
    sent(1)
    finish(1)

    def prepare_ends(y, carry):
        for e_x in (0, CX + 1):
            for e_z in range(0, CZ + 2, 2):
                source(e_x, y, e_z, e_z + 1)
        return carry

    def prepare_sides(x, carry):
        for e_y in (0, CY + 1):
            for e_z in range(0, CZ + 2, 2):
                source(x, e_y, e_z, e_z + 1)
        for e_y in range(1, CY + 1):
            source(x, e_y, 0, CZ + 1)
        return carry

    lax.fori_loop(0, CY + 2, prepare_ends, 0, unroll=3)
    lax.fori_loop(1, CX + 1, prepare_sides, 0, unroll=2)


def near_body(order_ref, points_ref, sources, targets, local, out_ref, totals):
    lane = iota((1, PTS), 1)
    square_eye = iota((PTS, PTS), 0) == iota((PTS, PTS), 1)

    def rows(n, size):
        x, y, z = n >> 4, (n >> 2) & 3, n & 3
        base = ext_index(x, y, z)
        parity = (x & 1) * 4 + (y & 1) * 2 + (z & 1)
        parent = (x >> 1) * 4 + (y >> 1) * 2 + (z >> 1)
        blocks = []
        for s_x in range(-1, 2):
            for s_y in range(-1, 2):
                for s_z in range(-1, 2):
                    blocks.append(base + s_x * ((CY + 2) * (CZ + 2)) + s_y * (CZ + 2) + s_z)
        left = targets[n, 0:size, :]
        eye = iota((size, PTS), 0) == iota((size, PTS), 1)
        total = jnp.zeros((size, PTS), jnp.float32)
        for at in range(0, 28, 2):
            right = []
            charge = []
            for b in (at, at + 1):
                if b < 27:
                    right.append(sources[blocks[b]])
                    charge.append(points_ref[blocks[b], 3:4, :])
                else:
                    right.append(sources[EXT + n])
                    charge.append(local[pl.ds(parity * 8 + parent, 1), :])
            square = jnp.dot(
                left, jnp.concatenate(right, axis=1), preferred_element_type=jnp.float32
            )
            weight = lax.rsqrt(square)
            for k, b in enumerate((at, at + 1)):
                part = weight[:, k * PTS : (k + 1) * PTS]
                if b == 13:
                    part = jnp.where(eye, 0.0, part)
                total = total + part * charge[k]
        return total

    def finish(g):
        for k in range(LINE):
            n = order_ref[0, g * LINE + k]
            sums = jnp.sum(totals[k], axis=1, keepdims=True)
            flat = jnp.sum(jnp.where(square_eye, sums, 0.0), axis=0, keepdims=True)
            out_ref[pl.ds(n, 1), :] = jnp.where(lane < order_ref[0, LEAF + n], flat, 0.0)

    def leaf_group(g, carry):
        def steps_of(k):
            return lax.div(order_ref[0, LEAF + order_ref[0, g * LINE + k]] + STEP - 1, STEP)

        most = steps_of(LINE - 1)
        alike = steps_of(LINE // 2 - 1) == most

        def together(lower, upper):
            finish(jnp.maximum(g - 1, 0))
            for k in range(LINE):
                size = lower if k < LINE // 2 else upper
                totals[k, 0:size, :] = rows(order_ref[0, g * LINE + k], size)

        def among(low, high):
            if high - low == 1:
                size = STEP * high
                if low == 0:
                    together(size, size)
                else:
                    pl.when(alike)(partial(together, size, size))
                    pl.when(~alike)(partial(together, size - STEP, size))
                return
            mid = (low + high) // 2
            pl.when(most <= mid)(partial(among, low, mid))
            pl.when(most > mid)(partial(among, mid, high))

        among(0, PTS // STEP)
        return carry

    lax.fori_loop(0, LEAF // LINE, leaf_group, 0)
    finish(LEAF // LINE - 1)


def gather_all(positions, charges, counts, up_inverse, down_inverse, inner_surface, outer_surface):
    wide = (CX + 2, CY + 2, CZ + 2, 4, PTS)
    return pl.pallas_call(
        gather_body,
        out_shape=(
            pltpu.VMEM(wide, jnp.float32),
            pltpu.VMEM((EXT + LEAF, FEATS, PTS), jnp.bfloat16),
            pltpu.VMEM((LEAF, PTS, FEATS), jnp.bfloat16),
            pltpu.VMEM((LEAF, 2 * TERMS), jnp.float32),
            pltpu.SMEM((1, 2 * LEAF), jnp.int32),
        ),
        in_specs=[anywhere()] * 7,
        out_specs=(whole(),) * 4 + (scalars(),),
        scratch_shapes=[
            pltpu.VMEM((CX + 4, CY + 4, CZ // 2 + 2, 1, 2 * TERMS), jnp.float32),
            pltpu.VMEM((3, LEAF, PTS), jnp.float32),
            pltpu.VMEM((LEAF, PTS), jnp.float32),
            pltpu.VMEM((1, LEAF), jnp.int32),
            pltpu.VMEM((TERMS, TERMS), jnp.float32),
            pltpu.VMEM((TERMS, TERMS), jnp.float32),
            pltpu.VMEM((3, TERMS), jnp.float32),
            pltpu.VMEM((3, TERMS), jnp.float32),
            pltpu.VMEM((LEAF, PTS), jnp.float32),
            pltpu.VMEM((PTS, 2 * TERMS), jnp.float32),
            pltpu.VMEM((98, PAIRS * TERMS, 2 * TERMS), jnp.bfloat16),
            pltpu.VMEM((108, 8, 2 * TERMS), jnp.float32),
            pltpu.VMEM((64, 8, 16, 2 * TERMS), jnp.bfloat16),
            pltpu.VMEM((4, PTS), jnp.float32),
            pltpu.VMEM((1, 2 * LEAF), jnp.int32),
            pltpu.SemaphoreType.DMA((8,)),
            pltpu.SemaphoreType.DMA((2, len(SIDES))),
            pltpu.SemaphoreType.DMA((2, len(SIDES))),
        ],
        compiler_params=pltpu.CompilerParams(
            collective_id=0, has_side_effects=True, vmem_limit_bytes=32 * 2**20
        ),
        name="gather",
    )(positions, charges, counts, up_inverse, down_inverse, inner_surface, outer_surface)


def potentials(order, points, sources, targets, local):
    return pl.pallas_call(
        near_body,
        out_shape=jax.ShapeDtypeStruct((LEAF, PTS), jnp.float32),
        in_specs=[scalars()] + [whole()] * 4,
        out_specs=whole(),
        scratch_shapes=[pltpu.VMEM((LINE, PTS, PTS), jnp.float32)],
        compiler_params=pltpu.CompilerParams(vmem_limit_bytes=32 * 2**20),
        name="potentials",
    )(order, points, sources, targets, local)


def per_device(positions, charges, counts, up_inverse, down_inverse, inner_surface, outer_surface):
    arguments = (
        jnp.transpose(positions, (1, 0, 2)),
        charges,
        counts.reshape(1, LEAF),
        up_inverse,
        down_inverse,
        inner_surface,
        outer_surface,
    )
    points, sources, targets, local, order = gather_all(
        *(pltpu.with_memory_space_constraint(member, pltpu.HBM) for member in arguments)
    )
    return potentials(order, points.reshape(EXT, 4, PTS), sources, targets, local)


def solution(mesh):
    in_specs = (
        P(("gx", "gy", "gz"), None, None),
        P(("gx", "gy", "gz"), None),
        P(("gx", "gy", "gz")),
        P(),
        P(),
        P(),
        P(),
    )
    out_specs = P(("gx", "gy", "gz"), None)
    return jax.shard_map(
        per_device, mesh=mesh, in_specs=in_specs, out_specs=out_specs, check_vma=False
    )
```

profile of v0, /device:TPU:1, one launch (start us, length us, event | category | flops | bytes accessed | tf_op | source)
XLA Modules:
  0.0 25.3 jit_solution(743134850741997966)
XLA Ops:
  0.0 12.7 %gather.1 = (f32[6,6,6,4,128]{4,3,2,1,0:T(4,128)S(1)}, bf16[280,32,128]{2,1,0:T(8,128)(2,1)S(1)}, bf16[64,128,32]{2,1,0:T(8,128)(2,1)S(1)}, f32[64,128]{1,0:T(8,128)S(1)}, s32[1,128]{1,0:T(1,128)S(4)}) custom-call(f32[3,64,128]{2,1,0:T(8,128)} %bitcast.4, f32[64,128]{1,0:T(8,128)} %charge_hbm.1, s32[1,64]{1,0:T(1,128)} %bitcast.5, f32[64,64]{1,0:T(8,128)} %up_hbm.1, ...), custom_call_target="tpu_custom_call" | custom-call | tf_op jit(solution)/shard_map/gather/pallas_call | solution.py:630
  12.8 12.6 %potentials.1 = f32[64,128]{1,0:T(8,128)} custom-call(s32[1,128]{1,0:T(1,128)S(4)} %get-tuple-element.10.order_ref, f32[216,4,128]{2,1,0:T(4,128)S(1)} %bitcast.3, bf16[280,32,128]{2,1,0:T(8,128)(2,1)S(1)} %get-tuple-element.12.sources, bf16[64,128,32]{2,1,0:T(8,128)(2,1)S(1)} %get-tuple-element.13.targets, f32[64,128]{1,0:T(8,128)S(1)} %get-tuple-element.14.local), custom_call_target="tpu_custom_call" | custom-call | tf_op jit(solution)/shard_map/potentials/pallas_call | solution.py:669
where the time goes:
time: 25.6 us; the launch traced here: 25.3 us
  Pallas kernels  25.3 us (99%)
    pallas_call x1, Pallas kernels, gather_all(): pl.pallas_call(gather_body, out_shape=(pltpu.VMEM(wide, jnp.float32), plt...  12.7 us
    pallas_call x1, Pallas kernels, potentials(): pl.pallas_call(near_body, out_shape=jax.ShapeDtypeStruct((LEAF, PTS), jnp...  12.6 us

commit v1 on v0

--- a/solution.py
+++ b/solution.py
@@ -272,37 +272,44 @@
     )
 
 
-def translate_part(weights, grouped, down_ref, local):
-    def product(places, parities):
-        lefts = []
-        rights = []
-        for n_x, n_y in places:
-            for lanes in range(2):
-                pieces = []
-                for kind in (0, 4, 2, 6):
-                    for parity in parities:
-                        at = (n_x + parity // 2) * 8 + n_y + parity % 2
-                        pieces.append(grouped[at, kind + lanes])
-                lefts.append(jnp.concatenate(pieces, axis=0))
-            at = (n_x * 7 + n_y) * 2
-            rights.append(jnp.concatenate([weights[at], weights[at + 1]], axis=1))
-        result = jnp.dot(
-            jnp.concatenate(lefts, axis=1),
-            jnp.concatenate(rights, axis=0),
-            preferred_element_type=jnp.float32,
-        )
-        for kind in range(4):
-            for k, parity in enumerate(parities):
-                at = (kind * len(parities) + k) * 16
-                sums[kind * 4 + parity].append(result[at : at + 16])
-
+def product(weights, grouped, sums, places, parities):
+    lefts = []
+    rights = []
+    for n_x, n_y in places:
+        for lanes in range(2):
+            pieces = []
+            for kind in (0, 4, 2, 6):
+                for parity in parities:
+                    at = (n_x + parity // 2) * 8 + n_y + parity % 2
+                    pieces.append(grouped[at, kind + lanes])
+            lefts.append(jnp.concatenate(pieces, axis=0))
+        at = (n_x * 7 + n_y) * 2
+        rights.append(jnp.concatenate([weights[at], weights[at + 1]], axis=1))
+    result = jnp.dot(
+        jnp.concatenate(lefts, axis=1),
+        jnp.concatenate(rights, axis=0),
+        preferred_element_type=jnp.float32,
+    )
+    for kind in range(4):
+        for k, parity in enumerate(parities):
+            at = (kind * len(parities) + k) * 16
+            sums[kind * 4 + parity].append(result[at : at + 16])
+
+
+def translate_inner(weights, grouped):
+    inner_shifts = range(1, 6)
     sums = [[] for _ in range(16)]
+    places = [(n_x, n_y) for n_x in inner_shifts for n_y in inner_shifts]
+    product(weights, grouped, sums, places, (0, 1, 2, 3))
+    return sums
+
+
+def translate_outer(sums, weights, grouped, down_ref, local):
     inner_shifts = range(1, 6)
-    product([(n_x, n_y) for n_x in inner_shifts for n_y in inner_shifts], (0, 1, 2, 3))
-    product([(0, n_y) for n_y in range(7)], (2, 3))
-    product([(6, n_y) for n_y in range(7)], (0, 1))
-    product([(n_x, 0) for n_x in inner_shifts], (1, 3))
-    product([(n_x, 6) for n_x in inner_shifts], (0, 2))
+    product(weights, grouped, sums, [(0, n_y) for n_y in range(7)], (2, 3))
+    product(weights, grouped, sums, [(6, n_y) for n_y in range(7)], (0, 1))
+    product(weights, grouped, sums, [(n_x, 0) for n_x in inner_shifts], (1, 3))
+    product(weights, grouped, sums, [(n_x, 6) for n_x in inner_shifts], (0, 2))
     total = jnp.concatenate([sum(rows[1:], rows[0]) for rows in sums], axis=0)
     total = total[:, : 2 * TERMS] + total[:, 2 * TERMS :]
     lower = total[:LEAF] + total[LEAF : 2 * LEAF]
@@ -525,7 +532,7 @@
     sent(0)
     finish(0)
     gather_part(wide_dens, raw, grouped)
-    translate_part(weights, grouped, down, local)
+    sums = translate_inner(weights, grouped)
     sent(1)
     finish(1)
 
@@ -543,8 +550,9 @@
             source(x, e_y, 0, CZ + 1)
         return carry
 
-    lax.fori_loop(0, CY + 2, prepare_ends, 0, unroll=3)
-    lax.fori_loop(1, CX + 1, prepare_sides, 0, unroll=2)
+    lax.fori_loop(0, CY + 2, prepare_ends, 0, unroll=CY + 2)
+    lax.fori_loop(1, CX + 1, prepare_sides, 0, unroll=CX)
+    translate_outer(sums, weights, grouped, down, local)
 
 
 def near_body(order_ref, points_ref, sources, targets, local, out_ref, totals):

time: 25.6 us -> 25.5 us (level)
    pallas_call x1, Pallas kernels: 12.6 us -> 12 us  [potentials(): pl.pallas_call(near_body, out_shape=jax.ShapeDtypeStruct((LEAF, PTS), jnp...]
    pallas_call x1, Pallas kernels: 12.7 us -> 13.1 us  [gather_all(): pl.pallas_call(gather_body, out_shape=(pltpu.VMEM(wide, jnp.float32), plt...]
where the time goes in v1:
time: 25.5 us; the launch traced here: 25.1 us
  Pallas kernels  25.1 us (98%)
    pallas_call x1, Pallas kernels, gather_all(): pl.pallas_call(gather_body, out_shape=(pltpu.VMEM(wide, jnp.float32), plt...  13.1 us
    pallas_call x1, Pallas kernels, potentials(): pl.pallas_call(near_body, out_shape=jax.ShapeDtypeStruct((LEAF, PTS), jnp...  12 us

profile of v1, /device:TPU:1, one launch (start us, length us, event | category | flops | bytes accessed | tf_op | source)
XLA Modules:
  0.0 25.1 jit_solution(16378932908022596841)
XLA Ops:
  0.0 13.1 %gather.1 = (f32[6,6,6,4,128]{4,3,2,1,0:T(4,128)S(1)}, bf16[280,32,128]{2,1,0:T(8,128)(2,1)S(1)}, bf16[64,128,32]{2,1,0:T(8,128)(2,1)S(1)}, f32[64,128]{1,0:T(8,128)S(1)}, s32[1,128]{1,0:T(1,128)S(4)}) custom-call(f32[3,64,128]{2,1,0:T(8,128)} %bitcast.4, f32[64,128]{1,0:T(8,128)} %charge_hbm.1, s32[1,64]{1,0:T(1,128)} %bitcast.5, f32[64,64]{1,0:T(8,128)} %up_hbm.1, ...), custom_call_target="tpu_custom_call" | custom-call | tf_op jit(solution)/shard_map/gather/pallas_call | solution.py:638
  13.1 12.0 %potentials.1 = f32[64,128]{1,0:T(8,128)} custom-call(s32[1,128]{1,0:T(1,128)S(4)} %get-tuple-element.10.order_ref, f32[216,4,128]{2,1,0:T(4,128)S(1)} %bitcast.3, bf16[280,32,128]{2,1,0:T(8,128)(2,1)S(1)} %get-tuple-element.12.sources, bf16[64,128,32]{2,1,0:T(8,128)(2,1)S(1)} %get-tuple-element.13.targets, f32[64,128]{1,0:T(8,128)S(1)} %get-tuple-element.14.local), custom_call_target="tpu_custom_call" | custom-call | tf_op jit(solution)/shard_map/potentials/pallas_call | solution.py:677
